TPU v7x, 32 devices: a whole 2x2x4 slice. The times are simulated.
32 devices in a mesh: modes: 4 (over y, core), gz: 8 (over z, x).
Axes of the slice: x: 2, y: 2, z: 4, core: 2. Of those that a mesh axis runs over, the one named last changes fastest.
Arguments:
- source_field: float32 [128, 2, 8, 2048], P('gz', None, None, 'modes'), may hold values from -0.075 to 0.075
- coupling_below: float32 [128], P('gz'), may hold values from 0.5 to 2
- coupling_above: float32 [128], P('gz'), may hold values from 0.5 to 2
- eigen_stream: float32 [8], replicated, may hold values from 0.000390625 to 0.015625
- eigen_span: float32 [2048], replicated, may hold values from 0.000390625 to 0.015625
Outputs:
- pressure: float32 [128, 2, 8, 2048], P('gz', None, 'modes')
All inputs are finite; a program needn't handle non-finite values.
Results may differ from a plain program's by a relative error of at most 0.0003.
Values sent between devices are 32-bit elements; how exact they have to be, the bound alone decides.
No kernel may reach another device: no remote copies, remote signals or barrier semaphores. Data moves between devices by JAX's collectives and lax.ppermute only.
A program may use at most 64 MiB of HBM per device.

v0:
```python
import jax
import jax.numpy as jnp
from jax import lax
from jax.sharding import PartitionSpec as P


def shifted(array, axis, by):
    count = lax.axis_size(axis)
    pairs = [(i, i + by) for i in range(count) if 0 <= i + by < count]
    return lax.ppermute(array, axis, pairs)


def thomas(lower_row, upper_row, spectral, sources, initial):
    row_count = sources.shape[0]

    def thomas_forward(carried, inputs):
        factor, partial_value = carried
        lower_val, upper_val, source_row = inputs
        pivots = lower_val + upper_val + spectral - lower_val * factor
        partial_value = (source_row + lower_val * partial_value) / pivots
        factor = upper_val / pivots
        return ((factor, partial_value), (factor, partial_value))

    _, (factors, partials) = lax.scan(
        thomas_forward,
        (jnp.zeros_like(spectral), initial),
        (lower_row, upper_row, sources),
        unroll=True,
    )
    retain = (jnp.arange(row_count) < row_count - 1).astype(jnp.float32)
    factors = factors * retain.reshape((row_count,) + (1,) * spectral.ndim)

    def thomas_backward(behind, inputs):
        factor, partial_value = inputs
        result = partial_value + factor * behind
        return (result, result)

    _, solved = lax.scan(
        thomas_backward, jnp.zeros_like(initial), (factors, partials), reverse=True, unroll=True
    )
    return solved


def reduced_solve(coeffs, right_side):

    def reduced_forward(carried, inputs):
        factor, partial_value = carried
        coeff_row, right_row = inputs
        pivots = coeff_row[1] - coeff_row[0] * factor
        factor = coeff_row[2] / pivots
        partial_value = (right_row - coeff_row[0] * partial_value) / pivots
        return ((factor, partial_value), (factor, partial_value))

    initial = (jnp.zeros_like(coeffs[0, 0]), jnp.zeros_like(right_side[0]))
    _, (factors, partials) = lax.scan(reduced_forward, initial, (coeffs, right_side), unroll=True)

    def reduced_backward(behind, inputs):
        factor, partial_value = inputs
        result = partial_value - factor * behind
        return (result, result)

    _, values = lax.scan(
        reduced_backward,
        jnp.zeros_like(right_side[0]),
        (factors, partials),
        reverse=True,
        unroll=True,
    )
    return values


def interfaces(planes, lower_row, upper_row, spectral):
    row_count = planes.shape[0]
    interior = row_count - 1
    modes_flat = planes.shape[2]
    last_mask = (jnp.arange(interior) == interior - 1).astype(jnp.float32) * upper_row[:interior]
    extra_source = last_mask[:, None, None] * jnp.ones((1, 1, modes_flat), jnp.float32)
    sources = jnp.concatenate(
        [planes[:interior], jnp.zeros((interior, 1, modes_flat), jnp.float32), extra_source], axis=1
    )
    initial = jnp.zeros((4, modes_flat), jnp.float32).at[2].set(1.0)
    solved = thomas(lower_row[:interior], upper_row[:interior], spectral, sources, initial)
    from_above = shifted(solved[0], "gz", -1)
    last_row = solved[interior - 1]
    lower_last = lower_row[row_count - 1]
    upper_last = upper_row[row_count - 1]
    coupling_down = -lower_last * last_row[2]
    central = (
        lower_last + upper_last + spectral - lower_last * last_row[3] - upper_last * from_above[2]
    )
    coupling_up = -upper_last * from_above[3]
    right_side = planes[row_count - 1] + lower_last * last_row[:2] + upper_last * from_above[:2]
    coeffs = jnp.stack([coupling_down, central, coupling_up])
    return (solved, coeffs, right_side)


def assemble(solved, interface_values):
    own_value = interface_values[:2]
    prev_value = interface_values[2:]
    inner = solved[:, :2] + solved[:, 2:3] * prev_value[None] + solved[:, 3:4] * own_value[None]
    return jnp.concatenate([inner, own_value[None]], axis=0)


def per_device(source_field, coupling_below, coupling_above, eigen_stream, eigen_span):
    arrived = lax.all_to_all(source_field, "modes", split_axis=2, concat_axis=3, tiled=True)
    row_count, _, kx_count, ky_count = arrived.shape
    partitions = lax.axis_size("gz")
    gz_index = lax.axis_index("gz")
    offset = lax.axis_index("modes") * kx_count
    stream_part = lax.dynamic_slice_in_dim(eigen_stream, offset, kx_count)
    spectral = stream_part[:, None] + eigen_span[None, :]
    global_row = gz_index * row_count + jnp.arange(row_count)
    lower_row = jnp.where(global_row == 0, 0.0, coupling_below)
    upper_row = jnp.where(global_row == row_count * partitions - 1, 0.0, coupling_above)
    modes_flat = kx_count * ky_count
    planes = arrived.reshape(row_count, 2, modes_flat)
    solved, coeffs, right_side = interfaces(planes, lower_row, upper_row, spectral.reshape(-1))
    coeff_items = coeffs.reshape(1, 3, kx_count, ky_count)
    right_items = right_side.reshape(1, 2, kx_count, ky_count)
    values = reduced_solve(
        lax.all_to_all(coeff_items, "gz", split_axis=3, concat_axis=0, tiled=True),
        lax.all_to_all(right_items, "gz", split_axis=3, concat_axis=0, tiled=True),
    )
    below_values = jnp.concatenate([jnp.zeros_like(values[:1]), values[:-1]], axis=0)
    paired = jnp.concatenate([values, below_values], axis=1)
    interface_values = lax.all_to_all(paired, "gz", split_axis=0, concat_axis=3, tiled=True)
    pressure = assemble(solved, interface_values.reshape(4, modes_flat))
    return pressure.reshape(row_count, 2, kx_count, ky_count)


def solution(mesh):
    in_specs = (P("gz", None, None, "modes"), P("gz"), P("gz"), P(), P())
    out_specs = P("gz", None, "modes", None)
    return jax.shard_map(
        per_device, mesh=mesh, in_specs=in_specs, out_specs=out_specs, check_vma=False
    )
```

profile of v0, /device:TPU:0, one launch (start us, length us, event | category | flops | bytes accessed | tf_op | source)
XLA Modules:
  0.0 153.8 jit_solution(18007086466472637981)
XLA Ops:
  0.0 2.2 %copy.91 = f32[16,2,8,512]{3,0,1,2:T(8,128)} copy(f32[16,2,8,512]{3,2,1,0:T(8,128)} %param.7) | data formatting | bytes 1048576 | tf_op args[0]
  2.2 4.3 %all-to-all-start = ((f32[16,2,8,512]{3,0,1,2:T(8,128)}), f32[16,2,8,512]{3,0,1,2:T(8,128)S(1)}, u32[]{:S(2)}, u32[]{:S(2)}) async-start(f32[16,2,8,512]{3,0,1,2:T(8,128)} %copy.91), calls=%async_computation | async-start | bytes 1048576 | tf_op jit(solution)/shard_map/all_to_all | solution.py:105
  31.2 17.7 %subtract_divide_fusion = (f32[1,4096]{1,0:T(1,128)S(1)}, f32[1,4096]{1,0:T(1,128)S(1)}, f32[1,4096]{1,0:T(1,128)S(1)}, f32[1,4096]{1,0:T(1,128)S(1)}, f32[1,409...) fusion(f32[1,4096]{1,0:T(1,128)S(1)} %bitcast.585, ...), kind=kLoop, calls=%fused_computation.174 | loop fusion | flops 172032 | bytes 475248 | tf_op jit(solution)/shard_map/eval_jaxpr/div | solution.py:21
  49.8 17.6 %multiply_subtract_fusion = (f32[4096]{0:T(1024)S(1)}, f32[4096]{0:T(1024)S(1)}, f32[4096]{0:T(1024)S(1)}, f32[4096]{0:T(1024)S(1)}, f32[4096]{0:T(1024)S(1)}, /...) fusion(f32[4096]{0:T(1024)S(1)} %bitcast.584, ...), kind=kLoop, calls=%fused_computation.160 | loop fusion | flops 172032 | bytes 475248 | tf_op jit(solution)/shard_map/eval_jaxpr/sub | solution.py:19
  69.1 9.6 %multiply_add_fusion = (f32[4,4096]{1,0:T(4,128)S(1)}, f32[4,4096]{1,0:T(4,128)S(1)}) fusion(f32[4096]{0:T(1024)S(1)} %bitcast.545, f32[4096]{0:T(1024)S(1)} %bitcast.554, f32[4096]{0:T(1024)S(1)} %bitcast.527, f32[4096]{0:T(1024)S(1)} %bitcast.556, f32[4096]{0:T(1024)S(1)} %bitcast.530, f32[4096]{0:T(1024)S(1)} %bitcast.558, f32[4096]{0:T(1024)S(1)} %bitcast.533, ...), kind=kLoop, calls=%fused_computation.56 | loop fusion | flops 1212416 | bytes 1671228 | tf_op jit(solution)/shard_map/eval_jaxpr/add | solution.py:35
  78.7 1.3 collective-permute-start
  80.0 10.3 %add_dynamic-update-slice_fusion = (f32[15,4,4096]{2,1,0:T(4,128)}, f32[1,4,4096]{2,1,0:T(4,128)S(1)}, f32[1,4,4096]{2,1,0:T(4,128)S(1)}, f32[1,4,4096]{2,1,0:T(...) fusion(f32[4096]{0:T(1024)S(1)} %bitcast.567, ...), kind=kLoop, calls=%fused_computation.57 | loop fusion | flops 1212415 | bytes 2457660
  97.9 1.2 constant_dynamic-update-slice_fusion.1
  99.1 1.4 fusion.53
  100.6 1.3 fusion.18
  102.0 1.1 copy.93
  103.1 3.5 %reshape.3546 = f32[8,1,1024]{2,1,0:T(1,128)} reshape(f32[2048,1,2,2]{3,2,1,0:T(2,128)S(1)} %bitcast.511) | data formatting | bytes 65536
  106.6 7.7 %all-to-all-start.1 = ((f32[8,1,1024]{2,1,0:T(1,128)}), f32[8,1,1024]{2,1,0:T(1,128)S(1)}, u32[]{:S(2)}, u32[]{:S(2)}) async-start(f32[8,1,1024]{2,1,0:T(1,128)} %reshape.3546), calls=%async_computation.1 | async-start | bytes 65536 | tf_op jit(solution)/shard_map/all_to_all | solution.py:122
  115.4 3.6 %reshape.3548 = f32[8,1,1536]{2,1,0:T(1,128)} reshape(f32[2048,1,2,3]{3,2,1,0:T(2,128)S(1)} %bitcast.512) | data formatting | bytes 98304
  119.0 1.9 %all-to-all-done.1 = f32[8,1,1024]{2,1,0:T(1,128)S(1)} async-done(((f32[8,1,1024]{2,1,0:T(1,128)}), f32[8,1,1024]{2,1,0:T(1,128)S(1)}, u32[]{:S(2)}, u32[]{:S(2)}) %all-to-all-start.1) | async-done | bytes 32800 | tf_op jit(solution)/shard_map/all_to_all | solution.py:122
  121.0 4.1 %all-to-all-start.2 = ((f32[8,1,1536]{2,1,0:T(1,128)}), f32[8,1,1536]{2,1,0:T(1,128)S(1)}, u32[]{:S(2)}, u32[]{:S(2)}) async-start(f32[8,1,1536]{2,1,0:T(1,128)} %reshape.3548), calls=%async_computation.2 | async-start | bytes 98304 | tf_op jit(solution)/shard_map/all_to_all | solution.py:121
  125.0 1.2 constant_dynamic-update-slice_fusion
  127.5 3.2 %reshape.3547 = f32[2048,1,2,2]{3,2,1,0:T(2,128)S(1)} reshape(f32[8,1024]{1,0:T(8,128)S(1)} %reduce.15) | data formatting | bytes 65536
  132.6 3.1 %reshape.3549 = f32[2048,1,2,3]{3,2,1,0:T(2,128)S(1)} reshape(f32[8,1536]{1,0:T(8,128)S(1)} %reduce.14) | data formatting | bytes 98304
  137.6 5.8 %all-to-all-start.3 = ((f32[8,4,2,256]{3,2,1,0:T(2,128)}), f32[8,4,2,256]{3,2,1,0:T(2,128)S(1)}, u32[]{:S(2)}, u32[]{:S(2)}) async-start(f32[8,4,2,256]{3,2,1,0:T(2,128)} %fusion.1), calls=%async_computation.3 | async-start | bytes 131072 | tf_op jit(solution)/shard_map/all_to_all | solution.py:126
  143.4 2.0 %fusion.112 = (f32[15,1,4096]{2,1,0:T(1,128)S(1)}, f32[15,1,4096]{2,1,0:T(1,128)S(1)}) fusion(f32[15,4,4096]{2,1,0:T(4,128)} %constant_dynamic-update-slice_fusion), kind=kLoop, calls=%fused_computation.270 | loop fusion | bytes 983040 | tf_op jit(solution)/shard_map/slice | solution.py:100
  145.8 4.5 %all-to-all-done.3 = f32[8,4,2,256]{3,2,1,0:T(2,128)S(1)} async-done(((f32[8,4,2,256]{3,2,1,0:T(2,128)}), f32[8,4,2,256]{3,2,1,0:T(2,128)S(1)}, u32[]{:S(2)}, u32[]{:S(2)}) %all-to-all-start.3) | async-done | bytes 65568 | tf_op jit(solution)/shard_map/all_to_all | solution.py:126
  150.5 1.6 %fusion = f32[15,2,4096]{2,1,0:T(2,128)S(1)} fusion(f32[15,4,4096]{2,1,0:T(4,128)} %constant_dynamic-update-slice_fusion, f32[2,4096]{1,0:T(2,128)S(1)} %mul.2749, f32[15,4096]{1,0:T(8,128)S(1)} %bitcast.519, f32[2,4096]{1,0:T(2,128)S(1)} %mul.2744, f32[15,4096]{1,0:T(8,128)S(1)} %bitcast.518), kind=kLoop, calls=%fused_computation.4 | loop fusion | flops 491520 | bytes 1540096 | tf_op jit(solution)/shard_map/add | solution.py:100
  152.6 1.1 pad_maximum_fusion.1
  (119 shorter events, 20.0 us)
Async XLA Ops:
  0.0 6.5 %copy-start.4 = (f32[16]{0:T(128)S(1)}, f32[16]{0:T(128)}, u32[]{:S(2)}) copy-start(f32[16]{0:T(128)} %param.9) | copy-start | bytes 196
  0.0 6.5 %copy-start.3 = (f32[16]{0:T(128)S(1)}, f32[16]{0:T(128)}, u32[]{:S(2)}) copy-start(f32[16]{0:T(128)} %param.8) | copy-start | bytes 196
  0.0 12.2 %copy-start.5 = (f32[8]{0:T(128)S(1)}, f32[8]{0:T(128)}, u32[]{:S(2)}) copy-start(f32[8]{0:T(128)} %param.10) | copy-start | bytes 100
  0.0 12.3 %copy-start.2 = (f32[2048]{0:T(1024)S(1)}, f32[2048]{0:T(1024)}, u32[]{:S(2)}) copy-start(f32[2048]{0:T(1024)} %param.11) | copy-start | bytes 24580
  2.2 65.2 %all-to-all-start = ((f32[16,2,8,512]{3,0,1,2:T(8,128)}), f32[16,2,8,512]{3,0,1,2:T(8,128)S(1)}, u32[]{:S(2)}, u32[]{:S(2)}) async-start(f32[16,2,8,512]{3,0,1,2:T(8,128)} %copy.91), calls=%async_computation | async-start | bytes 1048576 | tf_op jit(solution)/shard_map/all_to_all | solution.py:105
  67.8 1.3 copy-start.1
  68.4 11.6 %copy-start = (f32[1,4,4096]{2,1,0:T(4,128)S(1)}, f32[1,4,4096]{2,1,0:T(4,128)}, u32[]{:S(2)}) copy-start(f32[1,4,4096]{2,1,0:T(4,128)} %constant.75.clone.1) | copy-start | bytes 196612
  78.7 20.5 %collective-permute-start = (f32[4,4096]{1,0:T(4,128)S(1)}, f32[4,4096]{1,0:T(4,128)S(1)}, u32[]{:S(2)}, u32[]{:S(2)}) collective-permute-start(f32[4,4096]{1,0:T(4,128)S(1)} %get-tuple-element.64), channel_id=1, source_target_pairs={{1,0},{2,1},{3,2},{4,3},{5,4},{6,5},{7,6},{9,8},{10,9},{11,10},{12... | collective-permute-start | bytes 196616 | tf_op jit(solution)/shard_map/ppermute | solution.py:10
  106.6 14.4 %all-to-all-start.1 = ((f32[8,1,1024]{2,1,0:T(1,128)}), f32[8,1,1024]{2,1,0:T(1,128)S(1)}, u32[]{:S(2)}, u32[]{:S(2)}) async-start(f32[8,1,1024]{2,1,0:T(1,128)} %reshape.3546), calls=%async_computation.1 | async-start | bytes 65536 | tf_op jit(solution)/shard_map/all_to_all | solution.py:122
  121.0 10.9 %all-to-all-start.2 = ((f32[8,1,1536]{2,1,0:T(1,128)}), f32[8,1,1536]{2,1,0:T(1,128)S(1)}, u32[]{:S(2)}, u32[]{:S(2)}) async-start(f32[8,1,1536]{2,1,0:T(1,128)} %reshape.3548), calls=%async_computation.2 | async-start | bytes 98304 | tf_op jit(solution)/shard_map/all_to_all | solution.py:121
  137.6 12.7 %all-to-all-start.3 = ((f32[8,4,2,256]{3,2,1,0:T(2,128)}), f32[8,4,2,256]{3,2,1,0:T(2,128)S(1)}, u32[]{:S(2)}, u32[]{:S(2)}) async-start(f32[8,4,2,256]{3,2,1,0:T(2,128)} %fusion.1), calls=%async_computation.3 | async-start | bytes 131072 | tf_op jit(solution)/shard_map/all_to_all | solution.py:126
where the time goes:
time: 155 us; the launch traced here: 154 us
  other arithmetic  71 us (46%)
  local copies, waits for them, and re-layouts  30.6 us (20%)
  starting transfers between devices  23.1 us (15%)
  between operations  22.5 us (15%)
  waiting for transfers between devices  6.71 us (4%)
    unnamed x69, local copies, waits for them, and re-layouts  20.1 us
    div x1, other arithmetic, thomas_forward(): factor = upper_val / pivots  17.7 us
    sub x1, other arithmetic, thomas_forward(): pivots = lower_val + upper_val + spectral - lower_val * factor  17.6 us
    unnamed x12, other arithmetic  16.4 us
    add x1, other arithmetic, thomas_backward(): result = partial_value + factor * behind  9.6 us
    all_to_all x1, starting transfers between devices, per_device(): lax.all_to_all(right_items, 'gz', split_axis=3, concat_axis=0, tiled=True)  7.67 us
    all_to_all x1, starting transfers between devices, per_device(): lax.all_to_all(paired, 'gz', split_axis=0, concat_axis=3, tiled=True)  5.8 us
    all_to_all x1, waiting for transfers between devices, per_device(): lax.all_to_all(paired, 'gz', split_axis=0, concat_axis=3, tiled=True)  4.54 us
  transfers between devices with their start and end apart: 5, of which 3 were waited for; matrix products, arithmetic and copies ran while one was open for 47% of the time, Pallas kernels for 0%

commit v1 on v0

--- a/solution.py
+++ b/solution.py
@@ -119,7 +119,12 @@
     right_items = right_side.reshape(1, 2, kx_count, ky_count)
     values = reduced_solve(
         lax.all_to_all(coeff_items, "gz", split_axis=3, concat_axis=0, tiled=True),
-        lax.all_to_all(right_items, "gz", split_axis=3, concat_axis=0, tiled=True),
+        jnp.concatenate(
+            lax.all_to_all(
+                jnp.stack(jnp.split(right_items, lax.axis_size("gz"), axis=3)), "gz", 0, 0
+            ),
+            axis=0,
+        ),
     )
     below_values = jnp.concatenate([jnp.zeros_like(values[:1]), values[:-1]], axis=0)
     paired = jnp.concatenate([values, below_values], axis=1)

time: 155 us -> 144 us (0.929)
  local copies, waits for them, and re-layouts: 30.6 us -> 21.4 us
  other arithmetic: 71 us -> 63.8 us
  waiting for transfers between devices: 6.71 us -> 13.2 us
    unnamed x69 -> x74, local copies, waits for them, and re-layouts: 20.1 us -> 13.9 us
    all_to_all x1, waiting for transfers between devices: 0.21 us -> 6.2 us  [per_device(): lax.all_to_all(coeff_items, 'gz', split_axis=3, concat_axis=0, tiled=True)]
    unnamed x12, other arithmetic: 16.4 us -> 11.8 us
    all_to_all x1, starting transfers between devices: 7.67 us -> 3.52 us  [per_device(): lax.all_to_all(jnp.stack(jnp.split(right_items, lax.axis_size('gz'), axis...]
    all_to_all x1, starting transfers between devices: 4.06 us -> 7.67 us  [per_device(): lax.all_to_all(coeff_items, 'gz', split_axis=3, concat_axis=0, tiled=True)]
  transfers between devices with their start and end apart: 5 -> 5, of which waited for: 3 -> 3; matrix products, arithmetic and copies ran while one was open for 47% -> 40% of each run, Pallas kernels for 0% -> 0%
where the time goes in v1:
time: 144 us; the launch traced here: 142 us
  other arithmetic  63.8 us (44%)
  between operations  22.4 us (16%)
  starting transfers between devices  21.6 us (15%)
  local copies, waits for them, and re-layouts  21.4 us (15%)
  waiting for transfers between devices  13.2 us (9%)
    div x1, other arithmetic, thomas_forward(): factor = upper_val / pivots  17.7 us
    sub x1, other arithmetic, thomas_forward(): pivots = lower_val + upper_val + spectral - lower_val * factor  17.5 us
    unnamed x74, local copies, waits for them, and re-layouts  13.9 us
    unnamed x12, other arithmetic  11.8 us
    add x1, other arithmetic, thomas_backward(): result = partial_value + factor * behind  9.76 us
    all_to_all x1, starting transfers between devices, per_device(): lax.all_to_all(coeff_items, 'gz', split_axis=3, concat_axis=0, tiled=True)  7.67 us
    all_to_all x1, waiting for transfers between devices, per_device(): lax.all_to_all(coeff_items, 'gz', split_axis=3, concat_axis=0, tiled=True)  6.2 us
    all_to_all x1, waiting for transfers between devices, per_device(): lax.all_to_all(paired, 'gz', split_axis=0, concat_axis=3, tiled=True)  6.05 us
  transfers between devices with their start and end apart: 5, of which 3 were waited for; matrix products, arithmetic and copies ran while one was open for 40% of the time, Pallas kernels for 0%

profile of v1, /device:TPU:0, one launch (start us, length us, event | category | flops | bytes accessed | tf_op | source)
XLA Modules:
  0.0 142.3 jit_solution(15520847569386116250)
XLA Ops:
  0.0 2.2 %copy.88 = f32[16,2,8,512]{3,0,1,2:T(8,128)} copy(f32[16,2,8,512]{3,2,1,0:T(8,128)} %param.7) | data formatting | bytes 1048576 | tf_op args[0]
  2.2 4.3 %all-to-all-start = ((f32[16,2,8,512]{3,0,1,2:T(8,128)}), f32[16,2,8,512]{3,0,1,2:T(8,128)S(1)}, u32[]{:S(2)}, u32[]{:S(2)}) async-start(f32[16,2,8,512]{3,0,1,2:T(8,128)} %copy.88), calls=%async_computation | async-start | bytes 1048576 | tf_op jit(solution)/shard_map/all_to_all | solution.py:105
  6.5 0.7 fusion.116
  7.8 0.7 fusion.117
  12.2 0.7 divide_bitcast_fusion
  31.1 17.7 %subtract_divide_fusion = (f32[1,4096]{1,0:T(1,128)S(1)}, f32[1,4096]{1,0:T(1,128)S(1)}, f32[1,4096]{1,0:T(1,128)S(1)}, f32[1,4096]{1,0:T(1,128)S(1)}, f32[1,409...) fusion(f32[1,4096]{1,0:T(1,128)S(1)} %bitcast.608, ...), kind=kLoop, calls=%fused_computation.182 | loop fusion | flops 172032 | bytes 475248 | tf_op jit(solution)/shard_map/eval_jaxpr/div | solution.py:21
  49.8 17.5 %multiply_subtract_fusion = (f32[4096]{0:T(1024)S(1)}, f32[4096]{0:T(1024)S(1)}, f32[4096]{0:T(1024)S(1)}, f32[4096]{0:T(1024)S(1)}, f32[4096]{0:T(1024)S(1)}, /...) fusion(f32[4096]{0:T(1024)S(1)} %bitcast.607, ...), kind=kLoop, calls=%fused_computation.168 | loop fusion | flops 172032 | bytes 475248 | tf_op jit(solution)/shard_map/eval_jaxpr/sub | solution.py:19
  69.0 9.8 %multiply_add_fusion = (f32[4,4096]{1,0:T(4,128)S(1)}, f32[4,4096]{1,0:T(4,128)S(1)}) fusion(f32[4096]{0:T(1024)S(1)} %bitcast.571, f32[4096]{0:T(1024)S(1)} %bitcast.577, f32[4096]{0:T(1024)S(1)} %bitcast.553, f32[4096]{0:T(1024)S(1)} %bitcast.579, f32[4096]{0:T(1024)S(1)} %bitcast.556, f32[4096]{0:T(1024)S(1)} %bitcast.581, f32[4096]{0:T(1024)S(1)} %bitcast.559, ...), kind=kLoop, calls=%fused_computation.94 | loop fusion | flops 1212416 | bytes 1671228 | tf_op jit(solution)/shard_map/eval_jaxpr/add | solution.py:35
  78.7 1.3 collective-permute-start
  80.0 9.8 %constant_dynamic-update-slice_fusion.14 = (f32[15,4,4096]{2,1,0:T(4,128)S(1)}, f32[1,4,4096]{2,1,0:T(4,128)S(1)}, f32[1,4,4096]{2,1,0:T(4,128)S(1)}, f32[1,4,40...) fusion(f32[4096]{0:T(1024)S(1)} %bitcast.590, ...), kind=kLoop, calls=%fused_computation.39 | loop fusion | flops 1212415 | bytes 2457660
  91.6 1.2 fusion.18
  92.8 1.3 fusion.53
  98.4 1.1 copy.90
  99.5 3.6 %reshape.3547 = f32[8,1,1536]{2,1,0:T(1,128)} reshape(f32[2048,1,2,3]{3,2,1,0:T(2,128)S(1)} %bitcast.539) | data formatting | bytes 98304
  103.1 7.7 %all-to-all-start.2 = ((f32[8,1,1536]{2,1,0:T(1,128)}), f32[8,1,1536]{2,1,0:T(1,128)S(1)}, u32[]{:S(2)}, u32[]{:S(2)}) async-start(f32[8,1,1536]{2,1,0:T(1,128)} %reshape.3547), calls=%async_computation.2 | async-start | bytes 98304 | tf_op jit(solution)/shard_map/all_to_all | solution.py:121
  111.3 6.2 %all-to-all-done.2 = f32[8,1,1536]{2,1,0:T(1,128)S(1)} async-done(((f32[8,1,1536]{2,1,0:T(1,128)}), f32[8,1,1536]{2,1,0:T(1,128)S(1)}, u32[]{:S(2)}, u32[]{:S(2)}) %all-to-all-start.2) | async-done | bytes 49184 | tf_op jit(solution)/shard_map/all_to_all | solution.py:121
  117.5 3.5 %all-to-all-start.1 = ((f32[8,1,2,2,256]{4,3,2,1,0:T(2,128)}), f32[8,1,2,2,256]{4,3,2,1,0:T(2,128)S(1)}, u32[]{:S(2)}, u32[]{:S(2)}) async-start(f32[8,1,2,2,256]{4,3,2,1,0:T(2,128)} %constant_dynamic-update-slice_fusion.15), calls=%async_computation.1 | async-start | bytes 65536 | tf_op jit(solution)/shard_map/all_to_all | solution.py:123
  121.6 0.8 reduce.14
  122.3 3.1 %reshape.3548 = f32[2048,1,2,3]{3,2,1,0:T(2,128)S(1)} reshape(f32[8,1536]{1,0:T(8,128)S(1)} %reduce.14) | data formatting | bytes 98304
  125.5 0.8 copy.118
  126.6 1.0 all-to-all-done.1
  128.4 4.8 %all-to-all-start.3 = ((f32[8,4,2,256]{3,2,1,0:T(2,128)}), f32[8,4,2,256]{3,2,1,0:T(2,128)S(1)}, u32[]{:S(2)}, u32[]{:S(2)}) async-start(f32[8,4,2,256]{3,2,1,0:T(2,128)} %fusion.1), calls=%async_computation.3 | async-start | bytes 131072 | tf_op jit(solution)/shard_map/all_to_all | solution.py:131
  134.0 6.1 %all-to-all-done.3 = f32[8,4,2,256]{3,2,1,0:T(2,128)S(1)} async-done(((f32[8,4,2,256]{3,2,1,0:T(2,128)}), f32[8,4,2,256]{3,2,1,0:T(2,128)S(1)}, u32[]{:S(2)}, u32[]{:S(2)}) %all-to-all-start.3) | async-done | bytes 65568 | tf_op jit(solution)/shard_map/all_to_all | solution.py:131
  141.2 1.1 pad_maximum_fusion.1
  (122 shorter events, 12.9 us)
Async XLA Ops:
  0.0 6.5 %copy-start.4 = (f32[16]{0:T(128)S(1)}, f32[16]{0:T(128)}, u32[]{:S(2)}) copy-start(f32[16]{0:T(128)} %param.9) | copy-start | bytes 196
  0.0 6.5 %copy-start.3 = (f32[16]{0:T(128)S(1)}, f32[16]{0:T(128)}, u32[]{:S(2)}) copy-start(f32[16]{0:T(128)} %param.8) | copy-start | bytes 196
  0.0 12.1 %copy-start.5 = (f32[8]{0:T(128)S(1)}, f32[8]{0:T(128)}, u32[]{:S(2)}) copy-start(f32[8]{0:T(128)} %param.10) | copy-start | bytes 100
  0.0 12.2 %copy-start.2 = (f32[2048]{0:T(1024)S(1)}, f32[2048]{0:T(1024)}, u32[]{:S(2)}) copy-start(f32[2048]{0:T(1024)} %param.11) | copy-start | bytes 24580
  2.2 65.1 %all-to-all-start = ((f32[16,2,8,512]{3,0,1,2:T(8,128)}), f32[16,2,8,512]{3,0,1,2:T(8,128)S(1)}, u32[]{:S(2)}, u32[]{:S(2)}) async-start(f32[16,2,8,512]{3,0,1,2:T(8,128)} %copy.88), calls=%async_computation | async-start | bytes 1048576 | tf_op jit(solution)/shard_map/all_to_all | solution.py:105
  67.7 1.3 copy-start.1
  68.3 11.8 %copy-start = (f32[1,4,4096]{2,1,0:T(4,128)S(1)}, f32[1,4,4096]{2,1,0:T(4,128)}, u32[]{:S(2)}) copy-start(f32[1,4,4096]{2,1,0:T(4,128)} %constant.75.clone.1) | copy-start | bytes 196612
  78.7 12.9 %collective-permute-start = (f32[4,4096]{1,0:T(4,128)S(1)}, f32[4,4096]{1,0:T(4,128)S(1)}, u32[]{:S(2)}, u32[]{:S(2)}) collective-permute-start(f32[4,4096]{1,0:T(4,128)S(1)} %get-tuple-element.64), channel_id=1, source_target_pairs={{1,0},{2,1},{3,2},{4,3},{5,4},{6,5},{7,6},{9,8},{10,9},{11,10},{12... | collective-permute-start | bytes 196616 | tf_op jit(solution)/shard_map/ppermute | solution.py:10
  103.1 14.5 %all-to-all-start.2 = ((f32[8,1,1536]{2,1,0:T(1,128)}), f32[8,1,1536]{2,1,0:T(1,128)S(1)}, u32[]{:S(2)}, u32[]{:S(2)}) async-start(f32[8,1,1536]{2,1,0:T(1,128)} %reshape.3547), calls=%async_computation.2 | async-start | bytes 98304 | tf_op jit(solution)/shard_map/all_to_all | solution.py:121
  117.5 10.0 %all-to-all-start.1 = ((f32[8,1,2,2,256]{4,3,2,1,0:T(2,128)}), f32[8,1,2,2,256]{4,3,2,1,0:T(2,128)S(1)}, u32[]{:S(2)}, u32[]{:S(2)}) async-start(f32[8,1,2,2,256]{4,3,2,1,0:T(2,128)} %constant_dynamic-update-slice_fusion.15), calls=%async_computation.1 | async-start | bytes 65536 | tf_op jit(solution)/shard_map/all_to_all | solution.py:123
  128.4 11.7 %all-to-all-start.3 = ((f32[8,4,2,256]{3,2,1,0:T(2,128)}), f32[8,4,2,256]{3,2,1,0:T(2,128)S(1)}, u32[]{:S(2)}, u32[]{:S(2)}) async-start(f32[8,4,2,256]{3,2,1,0:T(2,128)} %fusion.1), calls=%async_computation.3 | async-start | bytes 131072 | tf_op jit(solution)/shard_map/all_to_all | solution.py:131
